TPU v7x, 32 devices: a whole 2x2x4 slice. The times are simulated.
32 devices in a mesh: groups: 2 (over x), seq: 16 (over z, y, core).
Axes of the slice: x: 2, y: 2, z: 4, core: 2. Of those that a mesh axis runs over, the one named last changes fastest.
Arguments:
- patches: bfloat16 [4096, 1176], P(('groups', 'seq')), parts along dimension 0, may hold values from -6 to 6
- row_owner: int32 [4096, 1], P(('groups', 'seq')), parts along dimension 0, may hold values from 0 to 15; in each aligned block of 128 rows (0 to 127, 128 to 255, ...) at most 16 rows name the same one
- window_slot: int32 [4096], P(('groups', 'seq')), parts along dimension 0, may hold values from 0 to 3
- w_patch: bfloat16 [1176, 1280], replicated, may hold values from -1 to 1
- vit_gain: float32 [1280], replicated, may hold values from 0.1 to 1.9
- w_qkv: bfloat16 [1280, 1920], replicated, may hold values from -1 to 1
- queries: bfloat16 [4096, 4096], P(('groups', 'seq')), parts along dimension 0, may hold values from -36 to 36
- new_kv: bfloat16 [4096, 1024], P(('groups', 'seq')), parts along dimension 0, may hold values from -6 to 6
- kv_cache: bfloat16 [2048, 16, 1024], P(('groups', 'seq')), parts along dimension 0, may hold values from -6 to 6
- block_table: int32 [32, 64], P(('groups', 'seq')), parts along dimension 0, may hold values from -1 to 1023, as said below
Outputs:
- vision_out: bfloat16 [4096, 640], P(('groups', 'seq')), parts along dimension 0
- attention_out: bfloat16 [4096, 4096], P(('groups', 'seq')), parts along dimension 0
There are 2 independent parts, one for each index of `groups`. A program takes and returns all parts, laid end to end along the dimension named above; an argument that names none is the same for every part. Nothing has to cross between parts.
Inputs may be any that keep to these rules, and one draw needn't show every extreme that they name: `row_owner`: in the rows of one device, each owner is named by at most 16 rows. `block_table`: block b is stored on device b // 64. Each row lists 8 or more distinct blocks, then -1 entries; at most 8 of a row's blocks lie on one device.
All inputs are finite; a program needn't handle non-finite values.
Results may differ from a plain program's by a relative error of at most 0.0093.
Values may be sent and summed in bfloat16 or wider, within the bound.
A program may use at most 64 MiB of HBM per device.

v0:
```python
import functools

import jax
import jax.numpy as jnp
from jax import lax
from jax.experimental import pallas as pl
from jax.experimental.pallas import tpu as pltpu
from jax.sharding import PartitionSpec as P

VHEADS = 8
VHD = 80
QHEADS = 32
KVH = 4
HD = 128
DEAD = -1e30


def embed_rows(patch_rows, w_patch, vit_gain):
    embedded = jnp.dot(patch_rows, w_patch, preferred_element_type=jnp.float32).astype(jnp.bfloat16)
    widened = lax.optimization_barrier(embedded).astype(jnp.float32)
    factor = lax.rsqrt(jnp.mean(widened * widened, axis=1, keepdims=True) + 1e-06)
    return (widened * factor * vit_gain).astype(jnp.bfloat16)


def window_attention(qkv_rows, windows):
    total_rows = qkv_rows.shape[0]
    inner_width = VHEADS * VHD
    query_heads = qkv_rows[:, :inner_width].reshape(total_rows, VHEADS, VHD)
    key_heads = qkv_rows[:, inner_width : 2 * inner_width].reshape(total_rows, VHEADS, VHD)
    value_heads = qkv_rows[:, 2 * inner_width :].reshape(total_rows, VHEADS, VHD)
    is_live = windows >= 0
    every_row = jnp.arange(total_rows)
    scores = jnp.einsum(
        "qhd,khd->hqk", query_heads, key_heads, preferred_element_type=jnp.float32
    ) * VHD ** (-0.5)
    allowed = (windows[:, None] == windows[None, :]) & is_live[None, :] | (
        every_row[:, None] == every_row[None, :]
    )
    scores = jnp.where(allowed[None], scores, -jnp.inf)
    highest = jnp.max(scores, axis=2, keepdims=True)
    weights = jnp.exp(scores - highest)
    totals = jnp.sum(weights, axis=2)
    blended = jnp.einsum(
        "hqk,khd->qhd",
        weights.astype(jnp.bfloat16),
        value_heads,
        preferred_element_type=jnp.float32,
    )
    pieces = (blended / totals.T[:, :, None]).reshape(total_rows, inner_width)
    return pieces.astype(jnp.bfloat16)


def span_kernel(slots, q_ref, fresh_ref, bias_ref, kv_ref, o_ref, held, sems):
    tokens = q_ref.shape[0]
    table_len, block_tokens = held.shape[0] - tokens // kv_ref.shape[1], kv_ref.shape[1]
    group_size = QHEADS // KVH
    width = held.shape[2]

    def copy_of(t):
        return pltpu.make_async_copy(kv_ref.at[slots[t]], held.at[t], sems.at[t])

    fresh_copy = pltpu.make_async_copy(
        fresh_ref, held.at[pl.ds(table_len, tokens // block_tokens)], sems.at[table_len]
    )
    fresh_copy.start()
    for t in range(table_len):
        copy_of(t).start()
    for t in range(table_len):
        copy_of(t).wait()
    fresh_copy.wait()
    keys = held.shape[0] * block_tokens
    rows = 2 * tokens
    causal = lax.broadcasted_iota(jnp.int32, (rows, keys), 1) - table_len * block_tokens <= lax.rem(
        lax.broadcasted_iota(jnp.int32, (rows, keys), 0), tokens
    )
    bias = jnp.where(causal, bias_ref[...], DEAD)
    for g in range(KVH):
        key_head = held[:, :, g * HD : (g + 1) * HD].reshape(keys, HD)
        value_head = held[:, :, width // 2 + g * HD : width // 2 + (g + 1) * HD].reshape(keys, HD)
        for pair in range(group_size // 2):
            first = g * group_size + 2 * pair
            query = jnp.concatenate(
                [q_ref[:, (first + i) * HD : (first + i + 1) * HD] for i in range(2)], axis=0
            )
            scores = lax.dot_general(
                query, key_head, (((1,), (1,)), ((), ())), preferred_element_type=jnp.float32
            ) * HD ** (-0.5) + bias
            highest = jnp.max(scores, axis=1, keepdims=True)
            weights = jnp.exp(scores - highest)
            totals = jnp.sum(weights, axis=1, keepdims=True)
            blended = jnp.dot(
                weights.astype(jnp.bfloat16), value_head, preferred_element_type=jnp.float32
            )
            out = (blended / totals).astype(jnp.bfloat16)
            for i in range(2):
                o_ref[:, (first + i) * HD : (first + i + 1) * HD] = out[i * tokens : (i + 1) * tokens]


def prompt_attention(queries, new_kv, delivered, slots, table_live):
    tokens = queries.shape[0]
    table_len = slots.shape[0]
    block_tokens, width = delivered.shape[1:]
    held_blocks = table_len + tokens // block_tokens
    bias = jnp.concatenate(
        [
            jnp.where(jnp.repeat(table_live, block_tokens), 0.0, DEAD),
            jnp.zeros((tokens,), jnp.float32),
        ]
    ).astype(jnp.float32)[None, :]
    return pl.pallas_call(
        span_kernel,
        out_shape=jax.ShapeDtypeStruct(queries.shape, jnp.bfloat16),
        grid_spec=pltpu.PrefetchScalarGridSpec(
            num_scalar_prefetch=1,
            in_specs=[
                pl.BlockSpec(memory_space=pltpu.VMEM),
                pl.BlockSpec(memory_space=pl.ANY),
                pl.BlockSpec(memory_space=pltpu.VMEM),
                pl.BlockSpec(memory_space=pl.ANY),
            ],
            out_specs=pl.BlockSpec(memory_space=pltpu.VMEM),
            scratch_shapes=[
                pltpu.VMEM((held_blocks, block_tokens, width), jnp.bfloat16),
                pltpu.SemaphoreType.DMA((table_len + 1,)),
            ],
        ),
        compiler_params=pltpu.CompilerParams(vmem_limit_bytes=40 << 20),
        name="span",
    )(slots, queries, new_kv.reshape(tokens // block_tokens, block_tokens, width), bias, delivered)


def route_kernel(
    devices,
    capacity,
    scale_dims,
    patches_hbm,
    owner_ref,
    window_ref,
    w_patch_hbm,
    gain_ref,
    w_qkv_hbm,
    queries_hbm,
    fresh_hbm,
    cache_hbm,
    table_ref,
    vision_ref,
    span_ref,
    patches,
    w_patch,
    w_qkv,
    cache,
    query,
    fresh,
    tables,
    picks,
    picks_smem,
    staged,
    spans,
    span_bias,
    outgoing,
    arrived,
    qkv,
    attended,
    returned,
    top,
    total,
    blend,
    load_sems,
    query_sems,
    pick_sem,
    table_send,
    table_recv,
    row_send,
    row_recv,
    span_send,
    span_recv,
    back_send,
    back_recv,
):
    vit, blocks_dev, block_tokens = scale_dims
    me = lax.axis_index("seq")
    tokens = fresh.shape[0]
    per_owner = tables.shape[1]
    chunk = per_owner * block_tokens
    inner = VHEADS * VHD
    group_rows = QHEADS // KVH * tokens
    kv_width = KVH * HD

    def peer(k):
        other = me
        bit = 1
        while bit < devices:
            if (k // bit) % 2:
                other = other + bit * (1 - 2 * ((me // bit) % 2))
            bit *= 2
        return other

    def remote(src, dst, send, recv, k):
        return pltpu.make_async_remote_copy(
            src_ref=src,
            dst_ref=dst,
            send_sem=send.at[k],
            recv_sem=recv.at[k],
            device_id={"seq": peer(k)},
            device_id_type=pl.DeviceIdType.MESH,
        )

    def table_copy(k):
        return remote(tables.at[0], tables.at[k], table_send, table_recv, k)

    def row_copy(k):
        rows = pl.ds(k * capacity, capacity)
        return remote(outgoing.at[rows], arrived.at[rows], row_send, row_recv, k)

    def span_copy(k):
        rows = pl.ds(k * chunk, chunk)
        return remote(staged.at[rows], spans.at[rows], span_send, span_recv, k)

    def back_copy(k):
        rows = pl.ds(k * capacity, capacity)
        return remote(attended.at[rows], returned.at[rows], back_send, back_recv, k)

    others = range(1, devices)
    tables[0] = jnp.concatenate(
        [
            jnp.broadcast_to(table_ref[...], (per_owner, table_ref.shape[1])),
            jnp.full((per_owner, HD - table_ref.shape[1]), -1, jnp.int32),
        ],
        axis=1,
    )
    pairs = (
        (patches_hbm, patches),
        (w_patch_hbm, w_patch),
        (cache_hbm, cache),
        (w_qkv_hbm, w_qkv),
        (fresh_hbm, fresh),
    )
    loads = [pltpu.make_async_copy(a, b, load_sems.at[i]) for i, (a, b) in enumerate(pairs)]
    for load in loads:
        load.start()
    query_loads = [
        pltpu.make_async_copy(
            queries_hbm.at[:, pl.ds(h * HD, HD)],
            query.at[pl.ds(h * tokens, tokens)],
            query_sems.at[h],
        )
        for h in range(QHEADS)
    ]
    for load in query_loads:
        load.start()

    barrier = pltpu.get_barrier_semaphore()
    for k in others:
        pl.semaphore_signal(
            barrier, inc=1, device_id={"seq": peer(k)}, device_id_type=pl.DeviceIdType.MESH
        )
    pl.semaphore_wait(barrier, devices - 1)
    for k in others:
        table_copy(k).start()

    for k in others:
        table_copy(k).wait()
    asked = tables[...].reshape(devices * per_owner, HD)
    first = me * blocks_dev
    hits = (asked >= first) & (asked < first + blocks_dev)
    before = (
        lax.broadcasted_iota(jnp.int32, (HD, HD), 0) < lax.broadcasted_iota(jnp.int32, (HD, HD), 1)
    )
    places = jnp.dot(
        jnp.where(hits, 1.0, 0.0).astype(jnp.bfloat16),
        jnp.where(before, 1.0, 0.0).astype(jnp.bfloat16),
        preferred_element_type=jnp.float32,
    ).astype(jnp.int32)
    turn = lax.rem(lax.broadcasted_iota(jnp.int32, asked.shape, 0), per_owner)
    local = jnp.sum(
        jnp.where(hits & (places == turn), (asked - first).astype(jnp.float32), 0.0),
        axis=1,
        keepdims=True,
    ).astype(jnp.int32)
    picks[...] = jnp.broadcast_to(local, picks.shape)
    pick_copy = pltpu.make_async_copy(picks, picks_smem, pick_sem)
    pick_copy.start()
    loads[2].wait()
    pick_copy.wait()

    def gather(k):
        target = staged if k else spans
        for s in range(per_owner):
            pick = jnp.clip(picks_smem[k * per_owner + s, 0], 0, blocks_dev - 1)
            target[pl.ds(k * chunk + s * block_tokens, block_tokens), :] = cache[pick]
        if k:
            span_copy(k).start()

    early, late = (devices // 2, devices // 2 + 1), (devices - 2, devices - 1)
    for k in early:
        gather(k)
    src_rows = owner_ref.shape[1]
    sublanes = lax.broadcasted_iota(jnp.int32, (HD, src_rows), 0)
    route = jnp.bitwise_xor(owner_ref[...], me)
    route_hits = sublanes == route
    upper = lax.broadcasted_iota(jnp.int32, (src_rows, src_rows), 0) < lax.broadcasted_iota(
        jnp.int32, (src_rows, src_rows), 1
    )
    earlier = jnp.dot(
        jnp.where(route_hits, 1.0, 0.0).astype(jnp.bfloat16),
        jnp.where(upper, 1.0, 0.0).astype(jnp.bfloat16),
        preferred_element_type=jnp.float32,
    )
    ranks = jnp.sum(jnp.where(route_hits, earlier, 0.0), axis=0, keepdims=True).astype(jnp.int32)
    slot_count = outgoing.shape[0]
    slot_hits = jnp.where(
        lax.broadcasted_iota(jnp.int32, (slot_count, src_rows), 0) == route * capacity + ranks,
        1.0,
        0.0,
    ).astype(jnp.bfloat16)
    flip = (((0,), (0,)), ((), ()))
    contract = (((1,), (1,)), ((), ()))
    loads[0].wait()
    loads[1].wait()
    embedded = (
        lax.dot_general(patches[...], w_patch[...], flip, preferred_element_type=jnp.float32)
        .astype(jnp.bfloat16)
        .astype(jnp.float32)
    )
    factor = lax.rsqrt(jnp.mean(embedded * embedded, axis=1, keepdims=True) + 1e-06)
    normed = (embedded * factor * gain_ref[...].reshape(1, vit)).astype(jnp.bfloat16)
    tags = jnp.where(sublanes == window_ref[...], 1.0, 0.0).astype(jnp.bfloat16)
    outgoing[:, 0:vit] = jnp.dot(slot_hits, normed, preferred_element_type=jnp.float32).astype(
        jnp.bfloat16
    )
    outgoing[:, vit:] = lax.dot_general(
        slot_hits, tags, contract, preferred_element_type=jnp.float32
    ).astype(jnp.bfloat16)
    for k in others:
        row_copy(k).start()
    arrived[0:capacity] = outgoing[0:capacity]
    for k in range(devices):
        if k not in early and k not in late:
            gather(k)
    own = tables[0]
    step = lax.broadcasted_iota(jnp.int32, (per_owner, HD), 1)
    for k in range(devices):
        first = peer(k) * blocks_dev
        mine = (own >= first) & (own < first + blocks_dev)
        count = jnp.sum(jnp.where(mine, 1.0, 0.0), axis=1, keepdims=True).astype(jnp.int32)
        span_bias[k] = jnp.where(step < count * block_tokens, 0.0, DEAD)

    loads[4].wait()
    for load in query_loads:
        load.wait()
    causal = lax.rem(
        lax.broadcasted_iota(jnp.int32, (group_rows, tokens), 0), tokens
    ) >= lax.broadcasted_iota(jnp.int32, (group_rows, tokens), 1)
    for g in range(KVH):
        rows = slice(g * group_rows, (g + 1) * group_rows)
        scores = lax.dot_general(
            query[rows], fresh[:, g * HD : (g + 1) * HD], contract, preferred_element_type=jnp.float32
        ) * HD ** (-0.5)
        scores = jnp.where(causal, scores, DEAD)
        highest = jnp.max(scores, axis=1, keepdims=True)
        weights = jnp.exp(scores - highest)
        top[rows] = jnp.broadcast_to(highest, (group_rows, HD))
        total[rows] = weights
        blend[rows] = jnp.dot(
            weights.astype(jnp.bfloat16),
            fresh[:, kv_width + g * HD : kv_width + (g + 1) * HD],
            preferred_element_type=jnp.float32,
        )

    for k in others:
        row_copy(k).wait()
    loads[3].wait()
    qkv[...] = jnp.dot(
        arrived[:, 0:vit], w_qkv[...], preferred_element_type=jnp.float32
    ).astype(jnp.bfloat16)
    marks = arrived[:, vit:]
    same = lax.dot_general(marks, marks, contract, preferred_element_type=jnp.float32)
    allowed = (same > 0.5) | (
        lax.broadcasted_iota(jnp.int32, same.shape, 0)
        == lax.broadcasted_iota(jnp.int32, same.shape, 1)
    )
    columns = lax.broadcasted_iota(jnp.int32, (slot_count, inner), 1)
    pieces = jnp.zeros((slot_count, inner), jnp.float32)
    for h in range(VHEADS):
        inside = (columns >= h * VHD) & (columns < (h + 1) * VHD)
        head_query = jnp.where(inside, qkv[:, 0:inner].astype(jnp.float32), 0.0).astype(jnp.bfloat16)
        scores = lax.dot_general(
            head_query, qkv[:, inner : 2 * inner], contract, preferred_element_type=jnp.float32
        ) * VHD ** (-0.5)
        scores = jnp.where(allowed, scores, DEAD)
        weights = jnp.exp(scores - jnp.max(scores, axis=1, keepdims=True))
        totals = jnp.sum(weights, axis=1, keepdims=True)
        blended = jnp.dot(
            weights.astype(jnp.bfloat16), qkv[:, 2 * inner :], preferred_element_type=jnp.float32
        )
        pieces = jnp.where(inside, blended / totals, pieces)
    attended[...] = pieces.astype(jnp.bfloat16)
    for k in others:
        back_copy(k).start()
    for k in late:
        gather(k)
    returned[0:capacity] = attended[0:capacity]

    def absorb(k, width):
        base = k * chunk
        bias = jnp.concatenate([span_bias[k + i, 0:1] for i in range(width)], axis=1)
        span = pl.ds(base, width * chunk)
        for g in range(KVH):
            rows = slice(g * group_rows, (g + 1) * group_rows)
            scores = lax.dot_general(
                query[rows],
                spans[span, g * HD : (g + 1) * HD],
                contract,
                preferred_element_type=jnp.float32,
            ) * HD ** (-0.5) + bias
            old = top[rows]
            highest = jnp.maximum(old, jnp.max(scores, axis=1, keepdims=True))
            shrink = jnp.exp(old - highest)
            parts = [
                jnp.exp(scores[:, i * chunk : (i + 1) * chunk] - highest) for i in range(width)
            ]
            summed = total[rows] * shrink
            for part in parts:
                summed = summed + part
            weights = jnp.concatenate([part.astype(jnp.bfloat16) for part in parts], axis=1)
            top[rows] = highest
            total[rows] = summed
            blend[rows] = blend[rows] * shrink + jnp.dot(
                weights,
                spans[span, kv_width + g * HD : kv_width + (g + 1) * HD],
                preferred_element_type=jnp.float32,
            )

    span_copy(1).wait()
    absorb(0, 2)
    for pair in range(1, devices // 2 - 1):
        span_copy(2 * pair).wait()
        span_copy(2 * pair + 1).wait()
        absorb(2 * pair, 2)
    for k in others:
        back_copy(k).wait()
    vision_ref[...] = lax.dot_general(
        slot_hits, returned[...], flip, preferred_element_type=jnp.float32
    ).astype(jnp.bfloat16)
    for k in late:
        span_copy(k).wait()
        absorb(k, 1)
    for h in range(QHEADS):
        rows = slice(h * tokens, (h + 1) * tokens)
        span_ref[:, h * HD : (h + 1) * HD] = (
            blend[rows] / jnp.sum(total[rows], axis=1, keepdims=True)
        ).astype(jnp.bfloat16)


def routed(
    devices, capacity, patches, row_owner, window_slot, w_patch, vit_gain, w_qkv, queries, new_kv,
    kv_cache, block_table,
):
    src_rows, patch = patches.shape
    vit = w_patch.shape[1]
    inner = VHEADS * VHD
    tokens, width = new_kv.shape
    blocks_dev, block_tokens, _ = kv_cache.shape
    per_owner = 2 * block_table.shape[1] // devices
    slot_count = devices * capacity
    keys = devices * per_owner * block_tokens
    rows = QHEADS * tokens
    bf16, f32 = jnp.bfloat16, jnp.float32
    vmem, anywhere = pl.BlockSpec(memory_space=pltpu.VMEM), pl.BlockSpec(memory_space=pl.ANY)
    dma = pltpu.SemaphoreType.DMA
    return pl.pallas_call(
        functools.partial(route_kernel, devices, capacity, (vit, blocks_dev, block_tokens)),
        out_shape=(
            jax.ShapeDtypeStruct((src_rows, inner), bf16),
            jax.ShapeDtypeStruct(queries.shape, bf16),
        ),
        in_specs=[
            anywhere, vmem, vmem, anywhere, vmem, anywhere, anywhere, anywhere, anywhere, vmem,
        ],
        out_specs=(vmem, vmem),
        scratch_shapes=[
            pltpu.VMEM((patch, src_rows), bf16),
            pltpu.VMEM((patch, vit), bf16),
            pltpu.VMEM((vit, 3 * inner), bf16),
            pltpu.VMEM(kv_cache.shape, bf16),
            pltpu.VMEM((rows, HD), bf16),
            pltpu.VMEM((tokens, width), bf16),
            pltpu.VMEM((devices, per_owner, HD), jnp.int32),
            pltpu.VMEM((devices * per_owner, HD), jnp.int32),
            pltpu.SMEM((devices * per_owner, HD), jnp.int32),
            pltpu.VMEM((keys, width), bf16),
            pltpu.VMEM((keys, width), bf16),
            pltpu.VMEM((devices, per_owner, HD), f32),
            pltpu.VMEM((slot_count, vit + HD), bf16),
            pltpu.VMEM((slot_count, vit + HD), bf16),
            pltpu.VMEM((slot_count, 3 * inner), bf16),
            pltpu.VMEM((slot_count, inner), bf16),
            pltpu.VMEM((slot_count, inner), bf16),
            pltpu.VMEM((rows, HD), f32),
            pltpu.VMEM((rows, HD), f32),
            pltpu.VMEM((rows, HD), f32),
            dma((5,)),
            dma((QHEADS,)),
            dma,
        ]
        + [dma((devices,))] * 8,
        compiler_params=pltpu.CompilerParams(
            collective_id=0, has_side_effects=True, vmem_limit_bytes=56 << 20
        ),
        name="route",
    )(
        patches.T, row_owner.reshape(1, src_rows), window_slot.reshape(1, src_rows), w_patch,
        vit_gain, w_qkv, queries, new_kv, kv_cache, block_table,
    )


def shards(
    patches,
    row_owner,
    window_slot,
    w_patch,
    vit_gain,
    w_qkv,
    queries,
    new_kv,
    kv_cache,
    block_table,
):
    devices = lax.axis_size("seq")
    capacity = 2 * patches.shape[0] // devices
    per_owner = 2 * block_table.shape[1] // devices
    whole_tiles = capacity % 16 == 0 and per_owner == 8 and per_owner * kv_cache.shape[1] == HD
    if whole_tiles and devices & (devices - 1) == 0 and new_kv.shape[0] == HD and block_table.shape[1] < HD:
        return routed(
            devices, capacity, patches, row_owner, window_slot, w_patch, vit_gain, w_qkv, queries,
            new_kv, kv_cache, block_table,
        )
    table_row = block_table[0]
    table_len = table_row.shape[0]
    blocks_dev = kv_cache.shape[0]
    per_owner = max(1, 2 * table_len // devices)
    is_live = table_row >= 0
    holder = jnp.where(is_live, table_row // blocks_dev, -1)
    local_block = jnp.where(is_live, table_row % blocks_dev, 0)
    before_entry = jnp.arange(table_len)[:, None] > jnp.arange(table_len)[None, :]
    same_holder = (holder[:, None] == holder[None, :]) & is_live[None, :] & before_entry
    holder_rank = jnp.sum(same_holder.astype(jnp.int32), axis=1)
    request_slot = jnp.where(is_live, holder * per_owner + holder_rank, devices * per_owner)
    slot_hits = request_slot[:, None] == jnp.arange(devices * per_owner)[None, :]
    wanted = jnp.sum(jnp.where(slot_hits, local_block[:, None], 0), axis=0).astype(jnp.int32)
    asked = lax.all_to_all(
        wanted.reshape(devices, per_owner), "seq", split_axis=0, concat_axis=0, tiled=True
    )
    fetched = kv_cache[asked]
    delivered = lax.all_to_all(fetched, "seq", split_axis=0, concat_axis=0, tiled=True)

    src_rows = patches.shape[0]
    capacity = max(1, 2 * src_rows // devices)
    slot_count = devices * capacity
    owner_ids = row_owner[:, 0]
    owner_hits = (owner_ids[:, None] == jnp.arange(devices)[None, :]).astype(jnp.bfloat16)
    strictly_lower = (jnp.arange(src_rows)[:, None] > jnp.arange(src_rows)[None, :]).astype(
        jnp.bfloat16
    )
    earlier = jnp.dot(strictly_lower, owner_hits, preferred_element_type=jnp.float32)
    ranks = jnp.sum(earlier * owner_hits.astype(jnp.float32), axis=1).astype(jnp.int32)
    target_slot = owner_ids * capacity + ranks
    row_hits = jnp.arange(slot_count)[:, None] == target_slot[None, :]
    window_buffer = jnp.sum(jnp.where(row_hits, window_slot[None, :] + 1, 0), axis=1) - 1
    normed = embed_rows(patches, w_patch, vit_gain)
    outgoing = jnp.dot(
        row_hits.astype(jnp.bfloat16), normed, preferred_element_type=jnp.float32
    ).astype(jnp.bfloat16)
    tag = jnp.broadcast_to(window_buffer.astype(jnp.bfloat16)[:, None], (slot_count, HD))
    outgoing, fetched = lax.optimization_barrier(
        (jnp.concatenate([outgoing, tag], axis=1), fetched)
    )
    arrived = lax.all_to_all(
        outgoing.reshape(devices, capacity, -1), "seq", split_axis=0, concat_axis=0, tiled=True
    ).reshape(slot_count, -1)
    vit = normed.shape[1]
    arrived_windows = arrived[:, vit].astype(jnp.int32)
    qkv_rows = jnp.dot(arrived[:, :vit], w_qkv, preferred_element_type=jnp.float32).astype(
        jnp.bfloat16
    )
    attended = window_attention(qkv_rows, arrived_windows)
    returned = lax.all_to_all(
        attended.reshape(devices, capacity, -1), "seq", split_axis=0, concat_axis=0, tiled=True
    )
    vision_out = jnp.dot(
        row_hits.T.astype(jnp.bfloat16),
        returned.reshape(slot_count, -1),
        preferred_element_type=jnp.float32,
    ).astype(jnp.bfloat16)
    slots = jnp.where(is_live, request_slot, 0).astype(jnp.int32)
    attention_out = prompt_attention(
        queries,
        new_kv,
        delivered.reshape((devices * per_owner,) + kv_cache.shape[1:]),
        slots,
        is_live,
    )
    return (vision_out, attention_out)


def solution(mesh):
    in_specs = (
        P(("groups", "seq"), None),
        P(("groups", "seq"), None),
        P(("groups", "seq")),
        P(),
        P(),
        P(),
        P(("groups", "seq"), None),
        P(("groups", "seq"), None),
        P(("groups", "seq"), None, None),
        P(("groups", "seq"), None),
    )
    out_specs = (P(("groups", "seq"), None), P(("groups", "seq"), None))
    return jax.shard_map(shards, mesh=mesh, in_specs=in_specs, out_specs=out_specs, check_vma=False)
```

profile of v0, /device:TPU:11, one launch (start us, length us, event | category | flops | bytes accessed | tf_op | source)
XLA Modules:
  0.0 134.4 jit_solution(15722418321027373926)
XLA Ops:
  0.6 129.9 %route.1 = (bf16[128,640]{1,0:T(8,128)(2,1)}, bf16[128,4096]{1,0:T(8,128)(2,1)}) custom-call(bf16[1176,128]{1,0:T(8,128)(2,1)} %bitcast.3, s32[1,128]{1,0:T(1,128)} %bitcast.4, s32[1,128]{1,0:T(1,128)} %bitcast.5, bf16[1176,1280]{1,0:T(8,128)(2,1)} %w_patch_hbm.1, f32[1280]{0:T(1024)} %gain_ref.1, bf16[1280,1920]{1,0:T(8,128)(2,1)} %w_qkv_hbm.1, ...), custom_call_target="tpu_custom_call" | custom-call | tf_op jit(solution)/shard_map/route/pallas_call | solution.py:471
  130.6 1.6 %copy.14 = bf16[128,640]{1,0:T(8,128)(2,1)} copy(bf16[128,640]{1,0:T(8,128)(2,1)} %get-tuple-element.4) | data formatting | bytes 327680
  132.2 2.3 %copy.15 = bf16[128,4096]{1,0:T(8,128)(2,1)} copy(bf16[128,4096]{1,0:T(8,128)(2,1)} %get-tuple-element.5) | data formatting | bytes 2097152
where the time goes:
time: 135 us; the launch traced here: 134 us
  Pallas kernels  130 us (96%)
  local copies, waits for them, and re-layouts  3.88 us (3%)
    pallas_call x1, Pallas kernels, routed(): pl.pallas_call(functools.partial(route_kernel, devices, capacity, (vit, b...  130 us
    unnamed x2, local copies, waits for them, and re-layouts  3.88 us

commit v1 on v0

--- a/solution.py
+++ b/solution.py
@@ -254,9 +254,49 @@
         pl.semaphore_signal(
             barrier, inc=1, device_id={"seq": peer(k)}, device_id_type=pl.DeviceIdType.MESH
         )
+    src_rows = owner_ref.shape[1]
+    patch = patches.shape[0]
+    whole = patch // HD * HD
+    rest = patch - whole
+    flip = (((0,), (0,)), ((), ()))
+    contract = (((1,), (1,)), ((), ()))
+    sublanes = lax.broadcasted_iota(jnp.int32, (HD, src_rows), 0)
+    route = jnp.bitwise_xor(owner_ref[...], me)
+    route_hits = sublanes == route
+    upper = lax.broadcasted_iota(jnp.int32, (src_rows, src_rows), 0) < lax.broadcasted_iota(
+        jnp.int32, (src_rows, src_rows), 1
+    )
+    earlier = jnp.dot(
+        jnp.where(route_hits, 1.0, 0.0).astype(jnp.bfloat16),
+        jnp.where(upper, 1.0, 0.0).astype(jnp.bfloat16),
+        preferred_element_type=jnp.float32,
+    )
+    ranks = jnp.sum(jnp.where(route_hits, earlier, 0.0), axis=0, keepdims=True).astype(jnp.int32)
+    slot_count = outgoing.shape[0]
+    slot_hits = jnp.where(
+        lax.broadcasted_iota(jnp.int32, (slot_count, src_rows), 0) == route * capacity + ranks,
+        1.0,
+        0.0,
+    ).astype(jnp.bfloat16)
+    tags = jnp.where(
+        lax.broadcasted_iota(jnp.int32, (HD - rest, src_rows), 0) == window_ref[...], 1.0, 0.0
+    ).astype(jnp.bfloat16)
+    loads[0].wait()
+    outgoing[:, 0:whole] = lax.dot_general(
+        slot_hits, patches[0:whole], (((1,), (1,)), ((), ())), preferred_element_type=jnp.float32
+    ).astype(jnp.bfloat16)
+    outgoing[:, whole:] = lax.dot_general(
+        slot_hits,
+        jnp.concatenate([patches[whole:patch], tags], axis=0),
+        contract,
+        preferred_element_type=jnp.float32,
+    ).astype(jnp.bfloat16)
+    arrived[0:capacity] = outgoing[0:capacity]
     pl.semaphore_wait(barrier, devices - 1)
     for k in others:
         table_copy(k).start()
+    for k in reversed(others):
+        row_copy(k).start()
 
     for k in others:
         table_copy(k).wait()
@@ -291,52 +331,11 @@
         if k:
             span_copy(k).start()
 
-    early, late = (devices // 2, devices // 2 + 1), (devices - 2, devices - 1)
-    for k in early:
+    far = devices // 2
+    for k in [far, far + 1] + list(range(devices // 4, far)) + list(range(far + 2, devices)):
         gather(k)
-    src_rows = owner_ref.shape[1]
-    sublanes = lax.broadcasted_iota(jnp.int32, (HD, src_rows), 0)
-    route = jnp.bitwise_xor(owner_ref[...], me)
-    route_hits = sublanes == route
-    upper = lax.broadcasted_iota(jnp.int32, (src_rows, src_rows), 0) < lax.broadcasted_iota(
-        jnp.int32, (src_rows, src_rows), 1
-    )
-    earlier = jnp.dot(
-        jnp.where(route_hits, 1.0, 0.0).astype(jnp.bfloat16),
-        jnp.where(upper, 1.0, 0.0).astype(jnp.bfloat16),
-        preferred_element_type=jnp.float32,
-    )
-    ranks = jnp.sum(jnp.where(route_hits, earlier, 0.0), axis=0, keepdims=True).astype(jnp.int32)
-    slot_count = outgoing.shape[0]
-    slot_hits = jnp.where(
-        lax.broadcasted_iota(jnp.int32, (slot_count, src_rows), 0) == route * capacity + ranks,
-        1.0,
-        0.0,
-    ).astype(jnp.bfloat16)
-    flip = (((0,), (0,)), ((), ()))
-    contract = (((1,), (1,)), ((), ()))
-    loads[0].wait()
-    loads[1].wait()
-    embedded = (
-        lax.dot_general(patches[...], w_patch[...], flip, preferred_element_type=jnp.float32)
-        .astype(jnp.bfloat16)
-        .astype(jnp.float32)
-    )
-    factor = lax.rsqrt(jnp.mean(embedded * embedded, axis=1, keepdims=True) + 1e-06)
-    normed = (embedded * factor * gain_ref[...].reshape(1, vit)).astype(jnp.bfloat16)
-    tags = jnp.where(sublanes == window_ref[...], 1.0, 0.0).astype(jnp.bfloat16)
-    outgoing[:, 0:vit] = jnp.dot(slot_hits, normed, preferred_element_type=jnp.float32).astype(
-        jnp.bfloat16
-    )
-    outgoing[:, vit:] = lax.dot_general(
-        slot_hits, tags, contract, preferred_element_type=jnp.float32
-    ).astype(jnp.bfloat16)
-    for k in others:
-        row_copy(k).start()
-    arrived[0:capacity] = outgoing[0:capacity]
-    for k in range(devices):
-        if k not in early and k not in late:
-            gather(k)
+    for k in range(devices // 4):
+        gather(k)
     own = tables[0]
     step = lax.broadcasted_iota(jnp.int32, (per_owner, HD), 1)
     for k in range(devices):
@@ -370,10 +369,24 @@
     for k in others:
         row_copy(k).wait()
     loads[3].wait()
-    qkv[...] = jnp.dot(
-        arrived[:, 0:vit], w_qkv[...], preferred_element_type=jnp.float32
-    ).astype(jnp.bfloat16)
-    marks = arrived[:, vit:]
+    loads[1].wait()
+    embedded = (
+        (
+            jnp.dot(arrived[:, 0:whole], w_patch[0:whole], preferred_element_type=jnp.float32)
+            + jnp.dot(
+                arrived[:, whole:patch], w_patch[whole:patch], preferred_element_type=jnp.float32
+            )
+        )
+        .astype(jnp.bfloat16)
+        .astype(jnp.float32)
+    )
+    factor = lax.rsqrt(jnp.mean(embedded * embedded, axis=1, keepdims=True) + 1e-06)
+    normed = (embedded * factor * gain_ref[...].reshape(1, vit)).astype(jnp.bfloat16)
+    qkv[...] = jnp.dot(normed, w_qkv[...], preferred_element_type=jnp.float32).astype(jnp.bfloat16)
+    marks = arrived[:, whole:]
+    marks = jnp.where(
+        lax.broadcasted_iota(jnp.int32, marks.shape, 1) >= rest, marks.astype(jnp.float32), 0.0
+    ).astype(jnp.bfloat16)
     same = lax.dot_general(marks, marks, contract, preferred_element_type=jnp.float32)
     allowed = (same > 0.5) | (
         lax.broadcasted_iota(jnp.int32, same.shape, 0)
@@ -397,11 +410,9 @@
     attended[...] = pieces.astype(jnp.bfloat16)
     for k in others:
         back_copy(k).start()
-    for k in late:
-        gather(k)
     returned[0:capacity] = attended[0:capacity]
 
-    def absorb(k, width):
+    def absorb(k, width, last=False):
         base = k * chunk
         bias = jnp.concatenate([span_bias[k + i, 0:1] for i in range(width)], axis=1)
         span = pl.ds(base, width * chunk)
@@ -423,33 +434,32 @@
             for part in parts:
                 summed = summed + part
             weights = jnp.concatenate([part.astype(jnp.bfloat16) for part in parts], axis=1)
-            top[rows] = highest
-            total[rows] = summed
-            blend[rows] = blend[rows] * shrink + jnp.dot(
+            blended = blend[rows] * shrink + jnp.dot(
                 weights,
                 spans[span, kv_width + g * HD : kv_width + (g + 1) * HD],
                 preferred_element_type=jnp.float32,
             )
+            if last:
+                out = (blended / jnp.sum(summed, axis=1, keepdims=True)).astype(jnp.bfloat16)
+                for i in range(QHEADS // KVH):
+                    h = g * (QHEADS // KVH) + i
+                    span_ref[:, h * HD : (h + 1) * HD] = out[i * tokens : (i + 1) * tokens]
+            else:
+                top[rows] = highest
+                total[rows] = summed
+                blend[rows] = blended
 
     span_copy(1).wait()
     absorb(0, 2)
-    for pair in range(1, devices // 2 - 1):
+    for pair in range(1, devices // 2):
         span_copy(2 * pair).wait()
         span_copy(2 * pair + 1).wait()
-        absorb(2 * pair, 2)
+        absorb(2 * pair, 2, pair == devices // 2 - 1)
     for k in others:
         back_copy(k).wait()
     vision_ref[...] = lax.dot_general(
         slot_hits, returned[...], flip, preferred_element_type=jnp.float32
     ).astype(jnp.bfloat16)
-    for k in late:
-        span_copy(k).wait()
-        absorb(k, 1)
-    for h in range(QHEADS):
-        rows = slice(h * tokens, (h + 1) * tokens)
-        span_ref[:, h * HD : (h + 1) * HD] = (
-            blend[rows] / jnp.sum(total[rows], axis=1, keepdims=True)
-        ).astype(jnp.bfloat16)
 
 
 def routed(
@@ -491,8 +501,8 @@
             pltpu.VMEM((keys, width), bf16),
             pltpu.VMEM((keys, width), bf16),
             pltpu.VMEM((devices, per_owner, HD), f32),
-            pltpu.VMEM((slot_count, vit + HD), bf16),
-            pltpu.VMEM((slot_count, vit + HD), bf16),
+            pltpu.VMEM((slot_count, patch // HD * HD + HD), bf16),
+            pltpu.VMEM((slot_count, patch // HD * HD + HD), bf16),
             pltpu.VMEM((slot_count, 3 * inner), bf16),
             pltpu.VMEM((slot_count, inner), bf16),
             pltpu.VMEM((slot_count, inner), bf16),

time: 135 us -> 127 us (0.941)
  Pallas kernels: 130 us -> 121 us
    pallas_call x1, Pallas kernels: 130 us -> 121 us  [routed(): pl.pallas_call(functools.partial(route_kernel, devices, capacity, (vit, b...]
where the time goes in v1:
time: 127 us; the launch traced here: 125 us
  Pallas kernels  121 us (95%)
  local copies, waits for them, and re-layouts  3.88 us (3%)
    pallas_call x1, Pallas kernels, routed(): pl.pallas_call(functools.partial(route_kernel, devices, capacity, (vit, b...  121 us
    unnamed x2, local copies, waits for them, and re-layouts  3.88 us

profile of v1, /device:TPU:11, one launch (start us, length us, event | category | flops | bytes accessed | tf_op | source)
XLA Modules:
  0.0 125.5 jit_solution(9082098937755579288)
XLA Ops:
  0.6 120.9 %route.1 = (bf16[128,640]{1,0:T(8,128)(2,1)}, bf16[128,4096]{1,0:T(8,128)(2,1)}) custom-call(bf16[1176,128]{1,0:T(8,128)(2,1)} %bitcast.3, s32[1,128]{1,0:T(1,128)} %bitcast.4, s32[1,128]{1,0:T(1,128)} %bitcast.5, bf16[1176,1280]{1,0:T(8,128)(2,1)} %w_patch_hbm.1, f32[1280]{0:T(1024)} %gain_ref.1, bf16[1280,1920]{1,0:T(8,128)(2,1)} %w_qkv_hbm.1, ...), custom_call_target="tpu_custom_call" | custom-call | tf_op jit(solution)/shard_map/route/pallas_call | solution.py:481
  121.6 1.6 %copy.14 = bf16[128,640]{1,0:T(8,128)(2,1)} copy(bf16[128,640]{1,0:T(8,128)(2,1)} %get-tuple-element.4) | data formatting | bytes 327680
  123.2 2.3 %copy.15 = bf16[128,4096]{1,0:T(8,128)(2,1)} copy(bf16[128,4096]{1,0:T(8,128)(2,1)} %get-tuple-element.5) | data formatting | bytes 2097152
